TPU v7x, 512 devices: a whole 4x4x16 slice. The times are simulated.
512 devices in a mesh: seq: 64 (over y, z), mp: 8 (over x, core).
Axes of the slice: x: 4, y: 4, z: 16, core: 2. Of those that a mesh axis runs over, the one named last changes fastest.
Arguments:
- byte_states: bfloat16 [16384, 1024], P('seq'), may hold values from -6 to 6
- outer_gain: float32 [1024], replicated, may hold values from 0.1 to 1.9
- mamba_input: bfloat16 [1024, 1024], P(None, 'mp'), may hold values from -0.1875 to 0.1875
- mamba_step: bfloat16 [1024, 1024], P(None, 'mp'), may hold values from -0.1875 to 0.1875
- decay_rate: float32 [1024], P('mp'), as said below
- mixer_weight: bfloat16 [1024, 1024], P('mp'), may hold values from -0.1875 to 0.1875
- boundaries: int32 [64, 128], P('seq'), may hold values from 0 to 256, as said below
- span_counts: int32 [64], replicated, may hold values from 1 to 128, as said below
- up_weight: bfloat16 [1024, 4096], P('seq', 'mp'), may hold values from -0.1875 to 0.1875
- up_bias: float32 [4096], P('mp'), may hold values from -5 to 5
- inner_gain: float32 [4096], replicated, as said below
- query_weight: bfloat16 [4096, 4096], P('seq', 'mp'), as said below
- key_weight: bfloat16 [4096, 1024], P('seq', 'mp'), as said below
- value_weight: bfloat16 [4096, 1024], P('seq', 'mp'), may hold values from -0.09375 to 0.09375
- return_weight: bfloat16 [4096, 1024], P('mp'), may hold values from -0.09375 to 0.09375
Outputs:
- joined: bfloat16 [16384, 1024], P('seq', 'mp')
Inputs may be any that keep to these rules, and one draw needn't show every extreme that they name: `boundaries`: row s lists the spans of shard s: its first span_counts[s] entries rise strictly from 0 and are byte positions within the shard; each span runs to the next entry, the last to the shard's end; the other entries equal 256. `span_counts`: the counts sum to 4096; some shard has exactly 128 spans. `decay_rate`: Positive. `inner_gain`: Positive. `query_weight`: Finite. `key_weight`: Finite.
All inputs are finite; a program needn't handle non-finite values.
Results may differ from a plain program's by a relative error of at most 0.01.
Values may be sent and summed in bfloat16 or wider, within the bound.
A program may use at most 64 MiB of HBM per device.

v0:
```python
import math
import jax
import jax.numpy as jnp
from jax import lax
from jax.sharding import PartitionSpec as P

HEADS = 32
KV_HEADS = 8
HEAD = 128
eps = 1e-05
masked = -1e30
far_index = 1073741824


def prefix(value, axis, join, neutral):
    count, mine = (lax.axis_size(axis), lax.axis_index(axis))
    pieces = jax.tree.map(lambda part: lax.all_gather(part, axis), value)
    so_far = jax.tree.map(
        lambda part, zero: jnp.full_like(part, 0) + jnp.asarray(zero, part.dtype), value, neutral
    )

    def lap(position, so_far):
        longer = join(so_far, jax.tree.map(lambda part: part[position], pieces))
        return jax.tree.map(lambda new, old: jnp.where(position < mine, new, old), longer, so_far)

    return lax.fori_loop(0, count - 1, lap, so_far)


def rms_scale(values, gain):
    values = values.astype(jnp.float32)
    return values * lax.rsqrt(jnp.mean(values * values, axis=-1, keepdims=True) + eps) * gain


def combine_pairs(earlier, later):
    return (earlier[0] * later[0], later[0] * earlier[1] + later[1])


def pick_table(table, wanted, seq_ids):
    return jnp.sum(jnp.where(seq_ids[None, :] == wanted[:, None], table[None, :], 0), axis=1)


def block_size(piece_rows, shard_rows):
    limit = max(1, 1024 // shard_rows)
    pieces = max(1, piece_rows // shard_rows)
    best_size = 1
    for candidate in range(1, limit + 1):
        if pieces % candidate == 0:
            best_size = candidate
    return min(piece_rows, best_size * shard_rows)


def on_device(
    byte_states,
    outer_gain,
    mamba_input,
    mamba_step,
    decay_rate,
    mixer_weight,
    boundaries,
    span_counts,
    up_weight,
    up_bias,
    inner_gain,
    query_weight,
    key_weight,
    value_weight,
    return_weight,
):
    shards = lax.axis_size("seq")
    own_shard = lax.axis_index("seq")
    own_lane = lax.axis_index("mp")
    rows_here = byte_states.shape[0]
    capacity = boundaries.shape[1]
    column_count = mamba_input.shape[1]
    kv_local = key_weight.shape[1] // HEAD
    group_size = HEADS // KV_HEADS
    offsets = jnp.cumsum(span_counts) - span_counts
    seq_ids = jnp.arange(shards, dtype=jnp.int32)
    own_offset = jnp.sum(jnp.where(seq_ids == own_shard, offsets, 0))
    own_count = jnp.sum(jnp.where(seq_ids == own_shard, span_counts, 0))
    normed = rms_scale(byte_states, outer_gain).astype(jnp.bfloat16)
    inputs = jnp.dot(normed, mamba_input, preferred_element_type=jnp.float32)
    step_sizes = jax.nn.softplus(jnp.dot(normed, mamba_step, preferred_element_type=jnp.float32))
    rate_steps = step_sizes * decay_rate
    decays = jnp.exp(-rate_steps)
    drives = jnp.sqrt(-jnp.expm1(-2.0 * rate_steps)) * inputs
    through, local_states = lax.associative_scan(combine_pairs, (decays, drives), axis=0)
    starting = (jnp.ones((column_count,), jnp.float32), jnp.zeros((column_count,), jnp.float32))
    arriving = prefix((through[-1], local_states[-1]), "seq", combine_pairs, starting)
    states = (local_states + through * arriving[1][None, :]).astype(jnp.bfloat16)
    partial_value = jnp.dot(states, mixer_weight, preferred_element_type=jnp.float32)
    mixed_sum = lax.psum(partial_value, "mp")
    encoded = (byte_states.astype(jnp.float32) + mixed_sum).astype(jnp.bfloat16)
    skip_part = lax.dynamic_slice_in_dim(encoded, own_lane * column_count, column_count, 1)
    own_marks = boundaries[0]
    pooled = encoded[jnp.minimum(own_marks, rows_here - 1)]
    local_slot = jnp.arange(capacity, dtype=jnp.int32)
    query_index = jnp.where(local_slot < own_count, own_offset + local_slot, -1)
    columns = pooled
    widened_sum = jnp.dot(
        columns,
        lax.all_gather(up_weight, "seq", axis=0, tiled=True),
        preferred_element_type=jnp.float32,
    )
    widened_share = (widened_sum + up_bias[None, :]).astype(jnp.bfloat16)
    widened = lax.all_gather(widened_share, "mp", axis=1, tiled=True)
    inner_normed = rms_scale(widened, inner_gain).astype(jnp.bfloat16)
    columns = inner_normed
    query_part = jnp.dot(
        columns,
        lax.all_gather(query_weight, "seq", axis=0, tiled=True),
        preferred_element_type=jnp.float32,
    )
    key_part = jnp.dot(
        columns,
        lax.all_gather(key_weight, "seq", axis=0, tiled=True),
        preferred_element_type=jnp.float32,
    )
    value_part = jnp.dot(
        columns,
        lax.all_gather(value_weight, "seq", axis=0, tiled=True),
        preferred_element_type=jnp.float32,
    )
    queries = query_part.astype(jnp.bfloat16)
    key_rows = key_part.astype(jnp.bfloat16)
    value_rows = value_part.astype(jnp.bfloat16)
    query_count = queries.shape[0]
    grouped = (
        queries.reshape(query_count, kv_local, group_size, HEAD)
        .transpose(1, 0, 2, 3)
        .reshape(kv_local, query_count * group_size, HEAD)
    )
    row_index = jnp.repeat(query_index, group_size)
    shard_rows = key_rows.shape[0]
    score_scale = 1.0 / math.sqrt(HEAD)

    def key_index(whole_index):
        holder = whole_index // shard_rows
        within = whole_index % shard_rows
        holder_offset = pick_table(offsets, holder, seq_ids)
        holder_count = pick_table(span_counts, holder, seq_ids)
        return jnp.where(within < holder_count, holder_offset + within, far_index)

    def attend_block(running, key_block, value_block, index_block):
        row_peak, denominator, weighted = running
        scores = (
            jnp.einsum("hqd,khd->hqk", grouped, key_block, preferred_element_type=jnp.float32)
            * score_scale
        )
        scores = jnp.where(index_block[None, None, :] <= row_index[None, :, None], scores, masked)
        new_peak = jnp.maximum(row_peak, jnp.max(scores, axis=2))
        shrink = jnp.exp(row_peak - new_peak)
        lifted = jnp.exp(scores - new_peak[:, :, None])
        denominator = denominator * shrink + jnp.sum(lifted, axis=2)
        weighted = weighted * shrink[:, :, None] + jnp.einsum(
            "hqk,khd->hqd",
            lifted.astype(jnp.bfloat16),
            value_block,
            preferred_element_type=jnp.float32,
        )
        return (new_peak, denominator, weighted)

    query_total = query_count * group_size
    initial = (
        jnp.full((kv_local, query_total), masked, jnp.float32),
        jnp.zeros((kv_local, query_total), jnp.float32),
        jnp.zeros((kv_local, query_total, HEAD), jnp.float32),
    )
    key_piece = lax.all_gather(key_rows, "seq", axis=0, tiled=True)
    value_piece = lax.all_gather(value_rows, "seq", axis=0, tiled=True)
    piece_rows = key_piece.shape[0]
    block_rows = block_size(piece_rows, shard_rows)
    turn_count = piece_rows // block_rows
    key_blocks = key_piece.reshape(turn_count, block_rows, kv_local, HEAD)
    value_blocks = value_piece.reshape(turn_count, block_rows, kv_local, HEAD)

    def one_turn(turn_index, inner_running):
        whole_index = turn_index * block_rows + jnp.arange(block_rows, dtype=jnp.int32)
        return attend_block(
            inner_running, key_blocks[turn_index], value_blocks[turn_index], key_index(whole_index)
        )

    row_peak, denominator, weighted = lax.fori_loop(0, turn_count, one_turn, initial)
    attended = (weighted / denominator[:, :, None]).astype(jnp.bfloat16)
    attended = (
        attended.reshape(kv_local, query_count, group_size, HEAD)
        .transpose(1, 0, 2, 3)
        .reshape(query_count, kv_local * group_size * HEAD)
    )
    projected = jnp.dot(attended, return_weight, preferred_element_type=jnp.float32)
    returned = lax.psum_scatter(
        projected.astype(jnp.bfloat16), "mp", scatter_dimension=1, tiled=True
    )
    positions = jnp.arange(rows_here, dtype=jnp.int32)
    live_slots = jnp.arange(capacity, dtype=jnp.int32) < own_count
    passed = jnp.sum(
        ((own_marks[None, :] <= positions[:, None]) & live_slots[None, :]).astype(jnp.int32), axis=1
    )
    return (skip_part.astype(jnp.float32) + returned[passed - 1].astype(jnp.float32)).astype(
        jnp.bfloat16
    )


def solution(mesh):
    in_specs = (
        P("seq", None),
        P(),
        P(None, "mp"),
        P(None, "mp"),
        P("mp"),
        P("mp", None),
        P("seq", None),
        P(),
        P("seq", "mp"),
        P("mp"),
        P(),
        P("seq", "mp"),
        P("seq", "mp"),
        P("seq", "mp"),
        P("mp", None),
    )
    out_specs = P("seq", "mp")
    return jax.shard_map(
        on_device, mesh=mesh, in_specs=in_specs, out_specs=out_specs, check_vma=False
    )
```

profile of v0, /device:TPU:8, one launch (start us, length us, event | category | flops | bytes accessed | tf_op | source)
XLA Modules:
  0.0 1139.2 jit_solution(18261109659851616036)
XLA Ops:
  7.4 1.3 fusion.32
  8.8 1.5 negate_exponential_fusion
  12.6 79.6 %all-gather.1 = f32[64,1,128]{2,1,0:T(1,128)S(1)} all-gather(f32[1,1,128]{2,1,0:T(1,128)S(1)} %add_bitcast_fusion), channel_id=1, replica_groups=mesh['seq'=64,'mp'=8] {'seq'}, dimensions={0}, use_global_device_ids=true | all-gather | bytes 33280 | tf_op jit(solution)/shard_map/all_gather | solution.py:17
  92.3 73.3 %all-gather = f32[64,1,128]{2,1,0:T(1,128)S(1)} all-gather(f32[1,1,128]{2,1,0:T(1,128)S(1)} %add_bitcast_fusion.1), channel_id=1, replica_groups=mesh['seq'=64,'mp'=8] {'seq'}, dimensions={0}, use_global_device_ids=true | all-gather | bytes 33280 | tf_op jit(solution)/shard_map/all_gather | solution.py:17
  165.6 2.6 while.34
  168.2 1.3 fusion.43
  170.2 73.0 %all-reduce.34.cloned.1.call-done = f32[256,1024]{1,0:T(8,128)} async-done(((f32[256,1024]{1,0:T(8,128)}), f32[256,1024]{1,0:T(8,128)}) %all-reduce.34.cloned.1.call-update) | async-done | bytes 1048592 | tf_op jit(solution)/shard_map/psum | solution.py:92
  243.2 1.4 fusion.35
  244.6 0.9 gather_fusion
  245.5 61.3 %all-gather.10.cloned.1.call-done = bf16[1024,512]{1,0:T(8,128)(2,1)} async-done(((bf16[16,512]{1,0:T(8,128)(2,1)}), bf16[1024,512]{1,0:T(8,128)(2,1)}) %all-gather.10.cloned.1.call-update) | async-done | bytes 1048592 | tf_op jit(solution)/shard_map/all_gather | solution.py:102
  306.7 2.2 fusion.31
  310.9 26.2 %all-gather.12.cloned.1.call-done = bf16[128,4096]{1,0:T(8,128)(2,1)} async-done(((bf16[128,512]{1,0:T(8,128)(2,1)}), bf16[128,4096]{1,0:T(8,128)(2,1)}) %all-gather.12.cloned.1.call-update) | async-done | bytes 1048592 | tf_op jit(solution)/shard_map/all_gather | solution.py:106
  337.1 1.6 fusion.28
  338.8 140.2 %all-gather.20.cloned.1.call-done = bf16[4096,128]{1,0:T(8,128)(2,1)} async-done(((bf16[64,128]{1,0:T(8,128)(2,1)}), bf16[4096,128]{1,0:T(8,128)(2,1)}) %all-gather.20.cloned.1.call-update) | async-done | bytes 1048592 | tf_op jit(solution)/shard_map/all_gather | solution.py:121
  478.9 2.7 convolution_convert_fusion.2
  481.7 136.0 %all-gather.14.cloned.1.call-done = bf16[4096,128]{1,0:T(8,128)(2,1)} async-done(((bf16[64,128]{1,0:T(8,128)(2,1)}), bf16[4096,128]{1,0:T(8,128)(2,1)}) %all-gather.14.cloned.1.call-update) | async-done | bytes 1048592 | tf_op jit(solution)/shard_map/all_gather | solution.py:116
  617.7 2.3 convolution_convert_fusion.3
  620.5 1.3 fusion.50
  622.5 1.9 add_select_fusion.3
  624.4 0.7 convert_reduce_fusion
  625.1 137.2 %all-gather.18.cloned.1.call-done = bf16[4096,512]{1,0:T(8,128)(2,1)} async-done(((bf16[64,512]{1,0:T(8,128)(2,1)}), bf16[4096,512]{1,0:T(8,128)(2,1)}) %all-gather.18.cloned.1.call-update) | async-done | bytes 4194320 | tf_op jit(solution)/shard_map/all_gather | solution.py:111
  762.2 3.0 convolution_convert_fusion.1
  765.3 135.9 %all-gather.22.cloned.1.call-done = bf16[8192,128]{1,0:T(8,128)(2,1)} async-done(((bf16[128,128]{1,0:T(8,128)(2,1)}), bf16[8192,128]{1,0:T(8,128)(2,1)}) %all-gather.22.cloned.1.call-update) | async-done | bytes 2097168 | tf_op jit(solution)/shard_map/all_gather | solution.py:170
  901.2 140.0 %all-gather.16.cloned.1.call-done = bf16[8192,128]{1,0:T(8,128)(2,1)} async-done(((bf16[128,128]{1,0:T(8,128)(2,1)}), bf16[8192,128]{1,0:T(8,128)(2,1)}) %all-gather.16.cloned.1.call-update) | async-done | bytes 2097168 | tf_op jit(solution)/shard_map/all_gather | solution.py:169
  1041.2 50.0 %while.35 = (s32[]{:T(128)}, f32[1,512]{1,0:T(1,128)S(1)}, f32[1,512]{1,0:T(1,128)S(1)}, f32[1,512,128]{2,1,0:T(8,128)S(1)}, s32[64]{0:T(128)S(1)}, /*index=5*/s...) while((s32[]{:T(128)}, f32[1,512]{1,0:T(1,128)S(1)}, ...), condition=%wide.region_13.14_spmd.clone, body=%wide.region_8.13_spmd.clone.sunk | while | flops 273186304 | bytes 7548097 | solution.py:183
  1041.2 0.8 fusion.77
  1042.0 0.7 broadcast_in_dim.150
  1042.9 2.0 fusion.78
  1046.0 1.5 fusion.82
  1047.5 0.8 fusion.77
  1048.3 0.7 broadcast_in_dim.150
  1049.2 2.0 fusion.78
  1051.2 0.7 fusion.79
  1052.2 1.5 fusion.82
  1053.7 0.8 fusion.77
  1054.5 0.7 broadcast_in_dim.150
  1055.4 2.0 fusion.78
  1057.4 0.7 fusion.79
  1058.5 1.5 fusion.82
  1060.0 0.8 fusion.77
  1060.8 0.7 broadcast_in_dim.150
  1061.7 2.0 fusion.78
  1064.7 1.5 fusion.82
  1066.2 0.8 fusion.77
  1067.0 0.7 broadcast_in_dim.150
  1067.9 2.0 fusion.78
  1071.0 1.5 fusion.82
  1072.5 0.8 fusion.77
  1073.3 0.7 broadcast_in_dim.150
  1074.1 2.0 fusion.78
  1077.2 1.5 fusion.82
  1078.7 0.8 fusion.77
  1079.5 0.7 broadcast_in_dim.150
  1080.4 2.0 fusion.78
  1083.5 1.5 fusion.82
  1085.0 0.8 fusion.77
  1085.8 0.7 broadcast_in_dim.150
  1086.6 2.0 fusion.78
  1089.7 1.5 fusion.82
  1091.8 0.8 copy.28
  1092.7 35.8 %reduce-scatter.4.cloned.1.call-done = bf16[128,128]{1,0:T(8,128)(2,1)} async-done(((bf16[1024,128]{1,0:T(8,128)(2,1)}), bf16[128,128]{1,0:T(8,128)(2,1)}) %reduce-scatter.4.cloned.1.call-update) | async-done | bytes 32784
  1128.5 0.9 copy.29
  1129.4 0.9 gather_fusion.1
  1130.3 1.5 add_convert_fusion
  (319 shorter events, 15.5 us)
Async XLA Ops:
  7.4 1084.1 %copy-start = (bf16[512,1024]{1,0:T(8,128)(2,1)S(1)}, bf16[512,1024]{1,0:T(8,128)(2,1)}, u32[]{:S(2)}) copy-start(bf16[512,1024]{1,0:T(8,128)(2,1)} %param.33) | copy-start | bytes 3145732
  7.4 3.0 copy-start.2
  7.4 3.0 copy-start.12
  7.4 3.0 copy-start.10
  7.4 235.8 %all-reduce.34.cloned.1.call-start = ((), (), s32[]{:S(2)}) async-start(), calls=%async_computation.1 | async-start | bytes 2097152 | tf_op jit(solution)/shard_map/psum | solution.py:92
  11.7 156.5 %copy-start.4 = (bf16[128,1024]{1,0:T(8,128)(2,1)S(1)}, bf16[128,1024]{1,0:T(8,128)(2,1)}, u32[]{:S(2)}) copy-start(bf16[128,1024]{1,0:T(8,128)(2,1)} %param.24) | copy-start | bytes 786436
  12.5 157.6 %copy-start.9 = (s32[1,128]{1,0:T(1,128)S(1)}, s32[1,128]{1,0:T(1,128)}, u32[]{:S(2)}) copy-start(s32[1,128]{1,0:T(1,128)} %param.25) | copy-start | bytes 1540
  169.5 137.2 %all-gather.10.cloned.1.call-start = ((), (), s32[]{:S(2)}) async-start(), calls=%async_computation.2 | async-start | bytes 1064960 | tf_op jit(solution)/shard_map/all_gather | solution.py:102
  170.1 167.0 %all-gather.12.cloned.1.call-start = ((), (), s32[]{:S(2)}) async-start(), calls=%async_computation.3 | async-start | bytes 1179648 | tf_op jit(solution)/shard_map/all_gather | solution.py:106
  170.2 136.5 %copy-start.8 = (f32[512]{0:T(512)S(1)}, f32[512]{0:T(512)}, u32[]{:S(2)}) copy-start(f32[512]{0:T(512)} %param.28) | copy-start | bytes 6148
  244.6 94.2 %copy-start.1 = (bf16[256,1024]{1,0:T(8,128)(2,1)}, bf16[256,1024]{1,0:T(8,128)(2,1)S(1)}, u32[]{:S(2)}) copy-start(bf16[256,1024]{1,0:T(8,128)(2,1)S(1)} %fusion.35) | copy-start | bytes 1572868
  244.6 234.3 %copy-start.11 = (f32[4096]{0:T(1024)S(1)}, f32[4096]{0:T(1024)}, u32[]{:S(2)}) copy-start(f32[4096]{0:T(1024)} %param.29) | copy-start | bytes 49156
  309.0 170.0 %all-gather.20.cloned.1.call-start = ((), (), s32[]{:S(2)}) async-start(), calls=%async_computation.7 | async-start | bytes 1064960 | tf_op jit(solution)/shard_map/all_gather | solution.py:121
  309.7 308.0 %all-gather.14.cloned.1.call-start = ((), (), s32[]{:S(2)}) async-start(), calls=%async_computation.4 | async-start | bytes 1064960 | tf_op jit(solution)/shard_map/all_gather | solution.py:116
  310.3 452.0 %all-gather.18.cloned.1.call-start = ((), (), s32[]{:S(2)}) async-start(), calls=%async_computation.6 | async-start | bytes 4259840 | tf_op jit(solution)/shard_map/all_gather | solution.py:111
  310.9 590.4 %all-gather.22.cloned.1.call-start = ((), (), s32[]{:S(2)}) async-start(), calls=%async_computation.8 | async-start | bytes 2129920 | tf_op jit(solution)/shard_map/all_gather | solution.py:170
  337.1 280.6 %copy-start.3 = (bf16[128,4096]{1,0:T(8,128)(2,1)S(1)}, bf16[128,4096]{1,0:T(8,128)(2,1)}, u32[]{:S(2)}) copy-start(bf16[128,4096]{1,0:T(8,128)(2,1)} %all-gather.12.cloned.1.call-done) | copy-start | bytes 3145732
  338.8 281.4 %copy-start.5 = (s32[64]{0:T(128)S(1)}, s32[64]{0:T(128)}, u32[]{:S(2)}) copy-start(s32[64]{0:T(128)} %param.26) | copy-start | bytes 772
  481.6 559.6 %all-gather.16.cloned.1.call-start = ((), (), s32[]{:S(2)}) async-start(), calls=%async_computation.5 | async-start | bytes 2129920 | tf_op jit(solution)/shard_map/all_gather | solution.py:169
  620.1 508.4 %reduce-scatter.4.cloned.1.call-start = ((), (), s32[]{:S(2)}) async-start(), calls=%async_computation.9 | async-start | bytes 294912
  1045.6 1.9 copy-start.6
  1051.8 1.9 copy-start.6
  1058.1 1.9 copy-start.6
  1064.3 1.9 copy-start.6
  1070.6 1.9 copy-start.6
  1076.8 1.9 copy-start.6
  1083.1 1.9 copy-start.6
  1089.3 1.9 copy-start.6
  1091.2 1.4 copy-start.7
Sparse Core Ops, SparseCore 0:
  169.7 73.5 all-reduce.33
  309.1 27.9 all-gather.11
  340.1 138.8 all-gather.19
  481.7 135.9 all-gather.13
  620.5 141.6 all-gather.17
  765.0 136.1 all-gather.21
  904.2 137.0 all-gather.15
  1092.8 35.7 reduce-scatter.3
Sparse Core Ops, SparseCore 1:
  173.0 133.7 all-gather.9
where the time goes:
time: 1140 us
  waiting for transfers between devices  888 us (78%)
  blocking collectives  153 us (13%)
  matrix products  41.2 us (4%)
  other arithmetic  27.3 us (2%)
  between operations  15.9 us (1%)
  local copies, waits for them, and re-layouts  11.6 us (1%)
    all_gather x2, blocking collectives, prefix(): pieces = jax.tree.map(lambda part: lax.all_gather(part, axis), value)  153 us
    all_gather x1, waiting for transfers between devices, on_device(): lax.all_gather(value_weight, 'seq', axis=0, tiled=True)  140 us
    all_gather x1, waiting for transfers between devices, on_device(): key_piece = lax.all_gather(key_rows, 'seq', axis=0, tiled=True)  140 us
    all_gather x1, waiting for transfers between devices, on_device(): lax.all_gather(query_weight, 'seq', axis=0, tiled=True)  137 us
    all_gather x1, waiting for transfers between devices, on_device(): lax.all_gather(key_weight, 'seq', axis=0, tiled=True)  136 us
    all_gather x1, waiting for transfers between devices, on_device(): value_piece = lax.all_gather(value_rows, 'seq', axis=0, tiled=True)  136 us
    psum x1, waiting for transfers between devices, on_device(): mixed_sum = lax.psum(partial_value, 'mp')  73 us
    all_gather x1, waiting for transfers between devices, on_device(): lax.all_gather(up_weight, 'seq', axis=0, tiled=True)  61.3 us
  transfers between devices with their start and end apart: 9, of which 9 were waited for; matrix products, arithmetic and copies ran while one was open for 1% of the time, Pallas kernels for 0%

commit v1 on v0

--- a/solution.py
+++ b/solution.py
@@ -166,8 +166,11 @@
         jnp.zeros((kv_local, query_total), jnp.float32),
         jnp.zeros((kv_local, query_total, HEAD), jnp.float32),
     )
-    key_piece = lax.all_gather(key_rows, "seq", axis=0, tiled=True)
-    value_piece = lax.all_gather(value_rows, "seq", axis=0, tiled=True)
+    key_piece, value_piece = jnp.split(
+        lax.all_gather(jnp.concatenate([key_rows, value_rows], axis=1), "seq", axis=0, tiled=True),
+        [key_rows.shape[1]],
+        axis=1,
+    )
     piece_rows = key_piece.shape[0]
     block_rows = block_size(piece_rows, shard_rows)
     turn_count = piece_rows // block_rows

time: 1140 us -> 994 us (0.87)
  waiting for transfers between devices: 888 us -> 753 us
  other arithmetic: 27.3 us -> 14.5 us
    all_gather x2 -> x1, waiting for transfers between devices: 276 us -> 140 us  [on_device(): lax.all_gather(jnp.concatenate([key_rows, value_rows], axis=1), 'seq', ax...]
    unnamed x10 -> x9, waiting for transfers between devices: 38.2 us -> 37 us
  transfers between devices with their start and end apart: 9 -> 8, of which waited for: 9 -> 8; matrix products, arithmetic and copies ran while one was open for 1% -> 1% of each run, Pallas kernels for 0% -> 0%
where the time goes in v1:
time: 994 us; the launch traced here: 993 us
  waiting for transfers between devices  753 us (76%)
  blocking collectives  153 us (15%)
  matrix products  35.5 us (4%)
  local copies, waits for them, and re-layouts  19.1 us (2%)
  between operations  15.9 us (2%)
  other arithmetic  14.5 us (1%)
    all_gather x2, blocking collectives, prefix(): pieces = jax.tree.map(lambda part: lax.all_gather(part, axis), value)  153 us
    all_gather x1, waiting for transfers between devices, on_device(): lax.all_gather(value_weight, 'seq', axis=0, tiled=True)  140 us
    all_gather x1, waiting for transfers between devices, on_device(): lax.all_gather(jnp.concatenate([key_rows, value_rows], axis=1), 'seq', ax...  140 us
    all_gather x1, waiting for transfers between devices, on_device(): lax.all_gather(query_weight, 'seq', axis=0, tiled=True)  139 us
    all_gather x1, waiting for transfers between devices, on_device(): lax.all_gather(key_weight, 'seq', axis=0, tiled=True)  137 us
    psum x1, waiting for transfers between devices, on_device(): mixed_sum = lax.psum(partial_value, 'mp')  73 us
    all_gather x1, waiting for transfers between devices, on_device(): lax.all_gather(up_weight, 'seq', axis=0, tiled=True)  61.3 us
    unnamed x9, waiting for transfers between devices  37 us
  transfers between devices with their start and end apart: 8, of which 8 were waited for; matrix products, arithmetic and copies ran while one was open for 1% of the time, Pallas kernels for 0%

profile of v1, /device:TPU:8, one launch (start us, length us, event | category | flops | bytes accessed | tf_op | source)
XLA Modules:
  0.0 993.0 jit_solution(1273104165054452454)
XLA Ops:
  7.4 1.3 fusion.32
  8.8 1.5 negate_exponential_fusion
  10.4 0.4 convolution_multiply_fusion
  12.6 79.6 %all-gather.1 = f32[64,1,128]{2,1,0:T(1,128)S(1)} all-gather(f32[1,1,128]{2,1,0:T(1,128)S(1)} %add_bitcast_fusion), channel_id=1, replica_groups=mesh['seq'=64,'mp'=8] {'seq'}, dimensions={0}, use_global_device_ids=true | all-gather | bytes 33280 | tf_op jit(solution)/shard_map/all_gather | solution.py:17
  92.3 73.3 %all-gather = f32[64,1,128]{2,1,0:T(1,128)S(1)} all-gather(f32[1,1,128]{2,1,0:T(1,128)S(1)} %add_bitcast_fusion.1), channel_id=1, replica_groups=mesh['seq'=64,'mp'=8] {'seq'}, dimensions={0}, use_global_device_ids=true | all-gather | bytes 33280 | tf_op jit(solution)/shard_map/all_gather | solution.py:17
  165.6 2.6 while.34
  168.2 1.3 fusion.43
  169.6 0.5 all-gather.9.cloned.1.call-update
  170.2 73.0 %all-reduce.34.cloned.1.call-done = f32[256,1024]{1,0:T(8,128)} async-done(((f32[256,1024]{1,0:T(8,128)}), f32[256,1024]{1,0:T(8,128)}) %all-reduce.34.cloned.1.call-update) | async-done | bytes 1048592 | tf_op jit(solution)/shard_map/psum | solution.py:92
  243.2 1.4 fusion.35
  244.6 0.9 gather_fusion
  245.5 61.3 %all-gather.9.cloned.1.call-done = bf16[1024,512]{1,0:T(8,128)(2,1)} async-done(((bf16[16,512]{1,0:T(8,128)(2,1)}), bf16[1024,512]{1,0:T(8,128)(2,1)}) %all-gather.9.cloned.1.call-update) | async-done | bytes 1048592 | tf_op jit(solution)/shard_map/all_gather | solution.py:102
  306.7 2.2 fusion.31
  309.0 0.7 all-gather.15.cloned.1.call-update
  309.7 0.5 all-gather.13.cloned.1.call-update
  310.3 0.5 all-gather.19.cloned.1.call-update
  310.9 26.2 %all-gather.11.cloned.1.call-done = bf16[128,4096]{1,0:T(8,128)(2,1)} async-done(((bf16[128,512]{1,0:T(8,128)(2,1)}), bf16[128,4096]{1,0:T(8,128)(2,1)}) %all-gather.11.cloned.1.call-update) | async-done | bytes 1048592 | tf_op jit(solution)/shard_map/all_gather | solution.py:106
  337.1 1.6 fusion.28
  338.7 140.2 %all-gather.15.cloned.1.call-done = bf16[4096,128]{1,0:T(8,128)(2,1)} async-done(((bf16[64,128]{1,0:T(8,128)(2,1)}), bf16[4096,128]{1,0:T(8,128)(2,1)}) %all-gather.15.cloned.1.call-update) | async-done | bytes 1048592 | tf_op jit(solution)/shard_map/all_gather | solution.py:121
  478.9 2.2 convolution_convert_fusion.2
  481.1 136.6 %all-gather.13.cloned.1.call-done = bf16[4096,128]{1,0:T(8,128)(2,1)} async-done(((bf16[64,128]{1,0:T(8,128)(2,1)}), bf16[4096,128]{1,0:T(8,128)(2,1)}) %all-gather.13.cloned.1.call-update) | async-done | bytes 1048592 | tf_op jit(solution)/shard_map/all_gather | solution.py:116
  617.7 1.8 convolution_convert_fusion.3
  619.6 0.6 pad_maximum_fusion.2
  620.6 0.7 fusion.50
  621.3 0.6 iota_compare_fusion.2
  621.9 1.2 add_select_fusion.3
  623.2 139.0 %all-gather.19.cloned.1.call-done = bf16[4096,512]{1,0:T(8,128)(2,1)} async-done(((bf16[64,512]{1,0:T(8,128)(2,1)}), bf16[4096,512]{1,0:T(8,128)(2,1)}) %all-gather.19.cloned.1.call-update) | async-done | bytes 4194320 | tf_op jit(solution)/shard_map/all_gather | solution.py:111
  762.2 2.9 convolution_convert_fusion.1
  765.3 139.6 %all-gather.17.cloned.1.call-done = bf16[8192,256]{0,1:T(8,128)(2,1)} async-done(((bf16[128,256]{0,1:T(8,128)(2,1)}), bf16[8192,256]{0,1:T(8,128)(2,1)}) %all-gather.17.cloned.1.call-update) | async-done | bytes 4194320 | tf_op jit(solution)/shard_map/all_gather | solution.py:170
  904.9 4.8 fusion.56
  909.7 4.1 copy.29
  913.8 4.1 copy.28
  917.8 29.2 %while.35 = (s32[]{:T(128)}, f32[1,512]{1,0:T(1,128)S(1)}, f32[1,512]{1,0:T(1,128)S(1)}, f32[1,512,128]{2,1,0:T(8,128)S(1)}, s32[64]{0:T(128)S(1)}, /*index=5*/s...) while((s32[]{:T(128)}, f32[1,512]{1,0:T(1,128)S(1)}, ...), condition=%wide.region_13.14_spmd.clone, body=%wide.region_8.13_spmd.clone.sunk | while | flops 273186304 | bytes 7546029 | solution.py:186
  918.2 1.4 fusion.79
  919.6 0.4 fusion.81
  920.0 1.5 fusion.83
  921.8 1.4 fusion.79
  923.3 0.4 fusion.81
  923.6 1.5 fusion.83
  925.5 1.4 fusion.79
  926.9 0.4 fusion.81
  927.3 1.5 fusion.83
  929.2 1.4 fusion.79
  930.6 0.4 fusion.81
  931.0 1.5 fusion.83
  932.8 1.4 fusion.79
  934.2 0.4 fusion.81
  934.6 1.5 fusion.83
  936.5 1.4 fusion.79
  937.9 0.4 fusion.81
  938.3 1.5 fusion.83
  940.1 1.4 fusion.79
  941.6 0.4 fusion.81
  941.9 1.5 fusion.83
  943.8 1.4 fusion.79
  945.2 0.4 fusion.81
  945.6 1.5 fusion.83
  947.1 0.1 divide_convert_fusion
  947.3 0.3 convolution_convert_fusion
  947.6 0.8 copy.30
  948.5 34.6 %reduce-scatter.4.cloned.1.call-done = bf16[128,128]{1,0:T(8,128)(2,1)} async-done(((bf16[1024,128]{1,0:T(8,128)(2,1)}), bf16[128,128]{1,0:T(8,128)(2,1)}) %reduce-scatter.4.cloned.1.call-update) | async-done | bytes 32784
  983.2 0.9 copy.31
  984.1 0.9 gather_fusion.1
  984.9 0.7 add_convert_fusion
  (300 shorter events, 6.5 us)
Async XLA Ops:
  7.4 939.9 %copy-start = (bf16[512,1024]{1,0:T(8,128)(2,1)S(1)}, bf16[512,1024]{1,0:T(8,128)(2,1)}, u32[]{:S(2)}) copy-start(bf16[512,1024]{1,0:T(8,128)(2,1)} %param.33) | copy-start | bytes 3145732
  7.4 3.0 copy-start.1
  7.4 3.0 copy-start.9
  7.4 3.0 copy-start.7
  7.4 235.8 %all-reduce.34.cloned.1.call-start = ((), (), s32[]{:S(2)}) async-start(), calls=%async_computation.1 | async-start | bytes 2097152 | tf_op jit(solution)/shard_map/psum | solution.py:92
  11.7 156.5 %copy-start.3 = (bf16[128,1024]{1,0:T(8,128)(2,1)S(1)}, bf16[128,1024]{1,0:T(8,128)(2,1)}, u32[]{:S(2)}) copy-start(bf16[128,1024]{1,0:T(8,128)(2,1)} %param.24) | copy-start | bytes 786436
  12.5 157.6 %copy-start.6 = (s32[1,128]{1,0:T(1,128)S(1)}, s32[1,128]{1,0:T(1,128)}, u32[]{:S(2)}) copy-start(s32[1,128]{1,0:T(1,128)} %param.25) | copy-start | bytes 1540
  169.5 137.2 %all-gather.9.cloned.1.call-start = ((), (), s32[]{:S(2)}) async-start(), calls=%async_computation.2 | async-start | bytes 1064960 | tf_op jit(solution)/shard_map/all_gather | solution.py:102
  170.1 167.0 %all-gather.11.cloned.1.call-start = ((), (), s32[]{:S(2)}) async-start(), calls=%async_computation.3 | async-start | bytes 1179648 | tf_op jit(solution)/shard_map/all_gather | solution.py:106
  170.2 136.5 %copy-start.5 = (f32[512]{0:T(512)S(1)}, f32[512]{0:T(512)}, u32[]{:S(2)}) copy-start(f32[512]{0:T(512)} %param.28) | copy-start | bytes 6148
  244.6 234.3 %copy-start.8 = (f32[4096]{0:T(1024)S(1)}, f32[4096]{0:T(1024)}, u32[]{:S(2)}) copy-start(f32[4096]{0:T(1024)} %param.29) | copy-start | bytes 49156
  308.9 170.0 %all-gather.15.cloned.1.call-start = ((), (), s32[]{:S(2)}) async-start(), calls=%async_computation.5 | async-start | bytes 1064960 | tf_op jit(solution)/shard_map/all_gather | solution.py:121
  309.7 308.0 %all-gather.13.cloned.1.call-start = ((), (), s32[]{:S(2)}) async-start(), calls=%async_computation.4 | async-start | bytes 1064960 | tf_op jit(solution)/shard_map/all_gather | solution.py:116
  310.3 452.0 %all-gather.19.cloned.1.call-start = ((), (), s32[]{:S(2)}) async-start(), calls=%async_computation.7 | async-start | bytes 4259840 | tf_op jit(solution)/shard_map/all_gather | solution.py:111
  310.8 594.1 %all-gather.17.cloned.1.call-start = ((), (), s32[]{:S(2)}) async-start(), calls=%async_computation.6 | async-start | bytes 4259840 | tf_op jit(solution)/shard_map/all_gather | solution.py:170
  337.1 280.6 %copy-start.2 = (bf16[128,4096]{1,0:T(8,128)(2,1)S(1)}, bf16[128,4096]{1,0:T(8,128)(2,1)}, u32[]{:S(2)}) copy-start(bf16[128,4096]{1,0:T(8,128)(2,1)} %all-gather.11.cloned.1.call-done) | copy-start | bytes 3145732
  338.7 281.6 %copy-start.4 = (s32[64]{0:T(128)S(1)}, s32[64]{0:T(128)}, u32[]{:S(2)}) copy-start(s32[64]{0:T(128)} %param.26) | copy-start | bytes 772
  620.2 363.0 %reduce-scatter.4.cloned.1.call-start = ((), (), s32[]{:S(2)}) async-start(), calls=%async_computation.8 | async-start | bytes 294912
Sparse Core Ops, SparseCore 0:
  169.6 73.5 all-reduce.33
  309.1 27.9 all-gather.10
  340.1 138.8 all-gather.14
  481.7 135.9 all-gather.12
  620.5 141.6 all-gather.18
  765.0 139.8 all-gather.16
  948.6 34.5 reduce-scatter.3
Sparse Core Ops, SparseCore 1:
  173.0 133.7 all-gather.8
